TPU v7x, 32 devices: a whole 2x2x4 slice. The times are simulated.
32 devices in a mesh: row: 4 (over z), col: 8 (over y, x, core).
Axes of the slice: x: 2, y: 2, z: 4, core: 2. Of those that a mesh axis runs over, the one named last changes fastest.
Arguments:
- tokens: bfloat16 [512, 8192], P('col', 'row'), may hold values from -6 to 6
- modality: int32 [512], P('row'), may hold values 0 or 1
- in_weight: bfloat16 [8192, 2, 28672], P('row', None, 'col'), may hold values from -0.0625 to 0.0625
- down_weight: bfloat16 [28672, 8192], P('col', 'row'), may hold values from -0.03125 to 0.03125
- d_mixed: bfloat16 [512, 8192], P('col', 'row'), may hold values from -6 to 6
Outputs:
- mixed: bfloat16 [512, 8192], P('col', 'row')
- d_down: bfloat16 [28672, 8192], P('col', 'row')
- d_in: bfloat16 [8192, 2, 28672], P('row', None, 'col')
- d_tokens: bfloat16 [512, 8192], P('col', 'row')
All inputs are finite; a program needn't handle non-finite values. No bound on the sum of `modality` on one device may be relied on, other than what follows from the above.
Results may differ from a plain program's by a relative error of at most 0.0049.
Values may be sent and summed in bfloat16 or wider, within the bound.
A program may use at most 192 MiB of HBM per device.

v0:
```python
import jax
import jax.numpy as jnp
from jax import lax
from jax.sharding import PartitionSpec as P


def exchange(partial, axis):
    count = lax.axis_size(axis)
    me = lax.axis_index(axis)
    rows = partial.shape[0] // count
    received = []
    for shift in range(1, count):
        start = lax.rem(me + shift, count) * rows
        block = lax.dynamic_slice_in_dim(partial, start, rows, 0).astype(jnp.bfloat16)
        moves = [(i, (i + shift) % count) for i in range(count)]
        received.append(lax.ppermute(block, axis, moves))
    total = lax.dynamic_slice_in_dim(partial, me * rows, rows, 0)
    for block in received:
        total = total + block.astype(jnp.float32)
    return total


def block_terms(rows, cotangents, in_weight, down_weight, spread):
    width = in_weight.shape[2]
    flat_in = in_weight.reshape(in_weight.shape[0], 2 * width)
    d_hidden = exchange(
        jnp.einsum("td,fd->tf", cotangents, down_weight, preferred_element_type=jnp.float32), "row"
    )
    projected = exchange(jnp.dot(rows, flat_in, preferred_element_type=jnp.float32), "row")
    gate_part = projected[:, :width]
    up_part = projected[:, width:]
    sigmoid_gate = jax.nn.sigmoid(gate_part)
    activated = gate_part * sigmoid_gate
    hidden = (activated * up_part).astype(jnp.bfloat16)
    d_gate = d_hidden * up_part * (sigmoid_gate + gate_part * sigmoid_gate * (1.0 - sigmoid_gate))
    d_local = jnp.concatenate([d_gate, d_hidden * activated], 1).astype(jnp.bfloat16)
    hidden_all = lax.all_gather(hidden, "row", axis=0, tiled=True)
    d_projected = lax.all_gather(d_local, "row", axis=0, tiled=True)
    mixed = lax.psum_scatter(
        jnp.dot(spread(hidden_all), down_weight, preferred_element_type=jnp.float32),
        "col",
        scatter_dimension=0,
        tiled=True,
    ).astype(jnp.bfloat16)
    d_down = jnp.einsum(
        "tf,td->fd", hidden_all, cotangents, preferred_element_type=jnp.float32
    ).astype(jnp.bfloat16)
    d_tokens = lax.psum_scatter(
        jnp.einsum("tk,dk->td", spread(d_projected), flat_in, preferred_element_type=jnp.float32),
        "col",
        scatter_dimension=0,
        tiled=True,
    ).astype(jnp.bfloat16)
    d_in = jnp.einsum("td,tk->dk", rows, d_projected, preferred_element_type=jnp.float32)
    d_in = lax.optimization_barrier(d_in.astype(jnp.bfloat16))
    return (mixed, d_down, d_in.reshape(in_weight.shape), d_tokens)


def per_device(tokens, modality, in_weight, down_weight, d_mixed):
    cotangent_all = lax.all_gather(d_mixed, "col", axis=0, tiled=True)
    rows_all = lax.all_gather(tokens, "col", axis=0, tiled=True)
    chosen = lax.all_gather(modality, "row", axis=0, tiled=True) == 1
    total = chosen.shape[0]
    place = jnp.cumsum(chosen.astype(jnp.int32)) - 1
    packed = total * 5 // 8

    def packed_form(rows, cotangents, w_in, w_down):
        pick = (chosen[None, :] & (place[None, :] == jnp.arange(packed)[:, None])).astype(
            jnp.bfloat16
        )
        take = lambda x: jnp.dot(pick, x, preferred_element_type=jnp.float32).astype(jnp.bfloat16)
        spread = lambda x: jnp.einsum(
            "ct,cf->tf", pick, x, preferred_element_type=jnp.float32
        ).astype(jnp.bfloat16)
        return block_terms(take(rows), take(cotangents), w_in, w_down, spread)

    def whole_form(rows, cotangents, w_in, w_down):
        keep = chosen[:, None].astype(jnp.bfloat16)
        return block_terms(rows * keep, cotangents * keep, w_in, w_down, lambda x: x)

    return lax.cond(
        place[-1] < packed, packed_form, whole_form, rows_all, cotangent_all, in_weight, down_weight
    )


def solution(mesh):
    return jax.shard_map(
        per_device,
        mesh=mesh,
        in_specs=(
            P("col", "row"),
            P("row"),
            P("row", None, "col"),
            P("col", "row"),
            P("col", "row"),
        ),
        out_specs=(P("col", "row"), P("col", "row"), P("row", None, "col"), P("col", "row")),
        check_vma=False,
    )
```

profile of v0, /device:TPU:0, one launch (start us, length us, event | category | flops | bytes accessed | tf_op | source)
XLA Modules:
  0.0 546.8 jit_solution(8745290950249474344)
XLA Ops:
  7.2 0.7 all-gather.16.cloned.1.call-update
  7.9 0.7 all-gather.18.cloned.1.call-update
  8.7 12.8 %all-gather = s32[4,1,128]{2,1,0:T(1,128)S(1)} all-gather(s32[1,1,128]{2,1,0:T(1,128)} %bitcast.47), channel_id=1, replica_groups=mesh['row'=4,'col'=8] {'row'}, dimensions={0}, use_global_device_ids=true | all-gather | bytes 2560 | tf_op jit(solution)/shard_map/all_gather | solution.py:62
  21.5 0.3 reduce-window.9
  21.8 0.1 slice.22
  21.9 0.1 slice_reduce_fusion
  22.1 0.6 slice.24
  23.3 17.1 %all-gather.16.cloned.1.call-done = bf16[512,2048]{1,0:T(8,128)(2,1)} async-done(((bf16[64,2048]{1,0:T(8,128)(2,1)}), bf16[512,2048]{1,0:T(8,128)(2,1)}) %all-gather.16.cloned.1.call-update) | async-done | bytes 2097168 | tf_op jit(solution)/shard_map/all_gather | solution.py:61
  40.4 29.7 %all-gather.18.cloned.1.call-done = bf16[512,2048]{1,0:T(8,128)(2,1)} async-done(((bf16[64,2048]{1,0:T(8,128)(2,1)}), bf16[512,2048]{1,0:T(8,128)(2,1)}) %all-gather.18.cloned.1.call-update) | async-done | bytes 2097168 | tf_op jit(solution)/shard_map/all_gather | solution.py:60
  70.1 468.5 %conditional.4 = (bf16[3584,2048]{1,0:T(8,128)(2,1)}, bf16[2048,2,3584]{2,1,0:T(2,128)(2,1)}, bf16[64,2048]{1,0:T(8,128)(2,1)S(1)}, bf16[64,2048]{1,0:T(8,128)(2,1)S(1)}) conditional(s32[]{:T(128)} %bitcast.3, (pred[512]{0:T(512)(128)(4,1)S(1)}, bf16[512,2048]{1,0:T(8,128)(2,1)}, bf16[2048,2,3584]{2,1,0:T(2,128)(2,1)}, bf16[512,2048]{1,0:T(8,128)(2,1)}, ...), branch_computations={%region_2.5_spmd, %region_5.8_spmd} | conditional | flops 67683221504 | bytes 523648416
  77.5 20.9 %copy.10 = bf16[256,8,2,3584]{3,1,2,0:T(8,128)(2,1)} copy(bf16[256,8,2,3584]{3,2,1,0:T(2,128)(2,1)} %bitcast.40) | data formatting | bytes 58720256
  98.4 0.8 convolution_convert_fusion.5
  99.2 1.1 copy-done.16
  100.3 14.7 %fusion.34 = f32[320,7168]{1,0:T(8,128)S(1)} fusion(bf16[320,2048]{1,0:T(8,128)(2,1)S(1)} %convolution_convert_fusion.5, bf16[2048,7168]{1,0:T(8,128)(2,1)} %bitcast.41), kind=kOutput, calls=%fused_computation.63 | convolution fusion | flops 9395240960 | bytes 39845888 | tf_op jit(solution)/shard_map/cond/branch_1_fun/dot_general | solution.py:29
  115.0 3.6 copy-done
  118.6 1.8 dynamic-slice_convert_fusion.8
  120.4 1.5 collective-permute-start.6
  121.9 2.3 collective-permute-start.8
  124.3 0.6 collective-permute-start.7
  124.9 2.0 convolution_convert_fusion.4
  126.8 8.6 %fusion.36 = f32[320,3584]{1,0:T(8,128)S(1)} fusion(bf16[320,2048]{1,0:T(8,128)(2,1)} %convolution_convert_fusion.4, bf16[3584,2048]{1,0:T(8,128)(2,1)} %get-tuple-element.49), kind=kOutput, calls=%fused_computation.65 | convolution fusion | flops 4697620480 | bytes 20578304 | tf_op jit(solution)/shard_map/cond/branch_1_fun/td,fd->tf/dot_general | solution.py:27
  135.4 2.1 copy-done.2
  137.5 1.3 dynamic-slice_convert_fusion.11
  138.8 1.5 collective-permute-start.9
  140.3 2.4 collective-permute-start.11
  142.6 8.1 %collective-permute-done.6 = bf16[80,7168]{1,0:T(8,128)(2,1)} collective-permute-done((bf16[80,7168]{1,0:T(8,128)(2,1)}, bf16[80,7168]{1,0:T(8,128)(2,1)}, u32[]{:S(2)}, u32[]{:S(2)}) %collective-permute-start.6) | collective-permute-done | bytes 1146912 | tf_op jit(solution)/shard_map/cond/branch_1_fun/ppermute | solution.py:16
  150.7 49.7 %collective-permute-start.10 = (bf16[80,3584]{1,0:T(8,128)(2,1)}, bf16[80,3584]{1,0:T(8,128)(2,1)S(1)}, u32[]{:S(2)}, u32[]{:S(2)}) collective-permute-start(bf16[80,3584]{1,0:T(8,128)(2,1)} %get-tuple-element.86), channel_id=1, source_target_pairs={{0,16},{8,24},{16,0},{24,8},{1,17},{9,25},{17,1},{25,9},{2,18},{10... | collective-permute-start | bytes 1720328 | tf_op jit(solution)/shard_map/cond/branch_1_fun/ppermute | solution.py:16
  200.4 47.9 %collective-permute-done.7 = bf16[80,7168]{1,0:T(8,128)(2,1)} collective-permute-done((bf16[80,7168]{1,0:T(8,128)(2,1)S(1)}, bf16[80,7168]{1,0:T(8,128)(2,1)}, u32[]{:S(2)}, u32[]{:S(2)}) %collective-permute-start.7) | collective-permute-done | bytes 1146912 | tf_op jit(solution)/shard_map/cond/branch_1_fun/ppermute | solution.py:16
  248.4 3.2 convert_add_fusion.2
  251.5 0.8 copy-done.3
  252.3 20.4 %collective-permute-done.10 = bf16[80,3584]{1,0:T(8,128)(2,1)S(1)} collective-permute-done((bf16[80,3584]{1,0:T(8,128)(2,1)}, bf16[80,3584]{1,0:T(8,128)(2,1)S(1)}, u32[]{:S(2)}, u32[]{:S(2)}) %collective-permute-start.10) | collective-permute-done | bytes 573472 | tf_op jit(solution)/shard_map/cond/branch_1_fun/ppermute | solution.py:16
  272.7 3.0 multiply_convert_fusion.4
  275.8 1.1 pad_maximum_fusion.1
  276.9 0.3 reduce-scatter.9.cloned.1.call-start
  277.2 45.8 %all-gather.12.cloned.1.call-done = bf16[320,3584]{1,0:T(8,128)(2,1)} async-done(((bf16[80,3584]{1,0:T(8,128)(2,1)}), bf16[320,3584]{1,0:T(8,128)(2,1)}) %all-gather.12.cloned.1.call-update) | async-done | bytes 2293776 | tf_op jit(solution)/shard_map/cond/branch_1_fun/all_gather | solution.py:37
  323.0 17.5 %fusion.11 = f32[512,2048]{1,0:T(8,128)} fusion(bf16[3584,2048]{1,0:T(8,128)(2,1)} %get-tuple-element.49, bf16[320,3584]{1,0:T(8,128)(2,1)} %all-gather.12.cloned.1.call-done, s32[512]{0:T(512)S(1)} %copy-done.9, pred[512]{0:T(512)(128)(4,1)S(1)} %copy-done.7), kind=kOutput, calls=%fused_computation.29 | convolution fusion | flops 8692760576 | bytes 21170688 | tf_op jit(solution)/shard_map/cond/branch_1_fun/dot_general | solution.py:40
  340.5 0.3 reduce-scatter.11.cloned.1.call-start
  340.8 70.2 %all-gather.14.cloned.1.call-done = bf16[320,7168]{1,0:T(8,128)(2,1)} async-done(((bf16[80,7168]{1,0:T(8,128)(2,1)}), bf16[320,7168]{1,0:T(8,128)(2,1)}) %all-gather.14.cloned.1.call-update) | async-done | bytes 4587536 | tf_op jit(solution)/shard_map/cond/branch_1_fun/all_gather | solution.py:38
  411.0 6.6 %convolution_convert_fusion.2.clone.4 = bf16[512,7168]{1,0:T(8,128)(2,1)S(1)} fusion(bf16[320,7168]{1,0:T(8,128)(2,1)} %all-gather.14.cloned.1.call-done, s32[512]{0:T(512)S(1)} %copy-done.9, pred[512]{0:T(512)(128)(4,1)S(1)} %copy-done.7), kind=kOutput, calls=%fused_computation.27.clone.clone.clone.1 | convolution fusion | flops 2352807936 | bytes 11930112 | tf_op jit(solution)/shard_map/cond/branch_1_fun/ct,cf->tf/dot_general | solution.py:72
  417.6 22.0 %fusion.12 = f32[512,2048]{1,0:T(8,128)} fusion(bf16[2048,7168]{1,0:T(8,128)(2,1)} %bitcast.42, bf16[512,7168]{1,0:T(8,128)(2,1)S(1)} %convolution_convert_fusion.2.clone.4), kind=kOutput, calls=%fused_computation.36 | convolution fusion | flops 15032385536 | bytes 40894464 | tf_op jit(solution)/shard_map/cond/branch_1_fun/tk,dk->td/dot_general | solution.py:49
  439.6 1.6 copy-done.10
  441.3 12.6 %fusion.35 = bf16[3584,2048]{1,0:T(8,128)(2,1)} fusion(bf16[320,3584]{1,0:T(8,128)(2,1)S(1)} %copy-done.10, bf16[320,2048]{1,0:T(8,128)(2,1)} %convolution_convert_fusion.4), kind=kOutput, calls=%fused_computation.64 | convolution fusion | flops 4697620480 | bytes 18284544 | tf_op jit(solution)/shard_map/cond/branch_1_fun/tf,td->fd/dot_general | solution.py:45
  453.9 19.5 %convolution_convert_fusion.1 = bf16[2048,7168]{1,0:T(8,128)(2,1)} fusion(bf16[320,2048]{1,0:T(8,128)(2,1)S(1)} %copy-done.17, bf16[320,7168]{1,0:T(8,128)(2,1)S(1)} %bitcast.49), kind=kOutput, calls=%fused_computation.26 | convolution fusion | flops 9409921024 | bytes 35258368 | tf_op jit(solution)/shard_map/cond/branch_1_fun/td,tk->dk/dot_general | solution.py:54
  473.4 62.7 %reshape.42 = bf16[2048,2,3584]{2,1,0:T(2,128)(2,1)} reshape(bf16[2048,7168]{1,0:T(8,128)(2,1)} %convolution_convert_fusion.1) | data formatting | bytes 58720256 | tf_op jit(solution)/shard_map/cond/branch_1_fun/reshape | solution.py:56
  536.1 1.1 convert_element_type.146
  537.2 1.1 convert_element_type.148
  538.6 0.7 copy-done.4
  539.3 0.1 copy-done.5
  (43 shorter events, 0.5 us)
Async XLA Ops:
  7.2 33.2 %all-gather.16.cloned.1.call-start = ((), (), s32[]{:S(2)}) async-start(), calls=%async_computation.12 | async-start | bytes 2359296 | tf_op jit(solution)/shard_map/all_gather | solution.py:61
  7.9 62.2 %all-gather.18.cloned.1.call-start = ((), (), s32[]{:S(2)}) async-start(), calls=%async_computation.13 | async-start | bytes 2359296 | tf_op jit(solution)/shard_map/all_gather | solution.py:60
  77.4 47.5 %copy-start.6 = (pred[512]{0:T(512)(128)(4,1)}, pred[512]{0:T(512)(128)(4,1)S(1)}, u32[]{:S(2)}) copy-start(pred[512]{0:T(512)(128)(4,1)S(1)} %get-tuple-element.44) | copy-start | bytes 1540
  77.4 47.5 %copy-start.8 = (s32[512]{0:T(512)}, s32[512]{0:T(512)S(1)}, u32[]{:S(2)}) copy-start(s32[512]{0:T(512)S(1)} %get-tuple-element.45) | copy-start | bytes 6148
  77.4 245.6 %all-gather.12.cloned.1.call-start = ((), (), s32[]{:S(2)}) async-start(), calls=%async_computation.8 | async-start | bytes 2867200 | tf_op jit(solution)/shard_map/cond/branch_1_fun/all_gather | solution.py:37
  77.5 20.9 %copy-start.13 = (bf16[512,2048]{1,0:T(8,128)(2,1)S(1)}, bf16[512,2048]{1,0:T(8,128)(2,1)}, u32[]{:S(2)}) copy-start(bf16[512,2048]{1,0:T(8,128)(2,1)} %get-tuple-element.46) | copy-start | bytes 6291460
  99.2 1.1 copy-start.16
  115.0 3.7 copy-start
  118.6 6.2 %copy-start.15 = (bf16[512,2048]{1,0:T(8,128)(2,1)S(1)}, bf16[512,2048]{1,0:T(8,128)(2,1)}, u32[]{:S(2)}) copy-start(bf16[512,2048]{1,0:T(8,128)(2,1)} %get-tuple-element.48) | copy-start | bytes 6291460
  120.4 30.3 %collective-permute-start.6 = (bf16[80,7168]{1,0:T(8,128)(2,1)}, bf16[80,7168]{1,0:T(8,128)(2,1)}, u32[]{:S(2)}, u32[]{:S(2)}) collective-permute-start(bf16[80,7168]{1,0:T(8,128)(2,1)} %get-tuple-element.79), channel_id=1, source_target_pairs={{0,8},{8,16},{16,24},{24,0},{1,9},{9,17},{17,25},{25,1},{2,10},{10... | collective-permute-start | bytes 3440648 | tf_op jit(solution)/shard_map/cond/branch_1_fun/ppermute | solution.py:16
  121.9 78.5 %collective-permute-start.8 = (bf16[80,7168]{1,0:T(8,128)(2,1)}, bf16[80,7168]{1,0:T(8,128)(2,1)}, u32[]{:S(2)}, u32[]{:S(2)}) collective-permute-start(bf16[80,7168]{1,0:T(8,128)(2,1)} %get-tuple-element.80), channel_id=1, source_target_pairs={{0,24},{8,0},{16,8},{24,16},{1,25},{9,1},{17,9},{25,17},{2,26},{10... | collective-permute-start | bytes 3440648 | tf_op jit(solution)/shard_map/cond/branch_1_fun/ppermute | solution.py:16
  124.3 124.1 %collective-permute-start.7 = (bf16[80,7168]{1,0:T(8,128)(2,1)S(1)}, bf16[80,7168]{1,0:T(8,128)(2,1)}, u32[]{:S(2)}, u32[]{:S(2)}) collective-permute-start(bf16[80,7168]{1,0:T(8,128)(2,1)S(1)} %get-tuple-element.81), channel_id=1, source_target_pairs={{0,16},{8,24},{16,0},{24,8},{1,17},{9,25},{17,1},{25,9},{2,18},{10... | collective-permute-start | bytes 3440648 | tf_op jit(solution)/shard_map/cond/branch_1_fun/ppermute | solution.py:16
  135.4 2.1 copy-start.2
  138.8 112.7 %collective-permute-start.9 = (bf16[80,3584]{1,0:T(8,128)(2,1)}, bf16[80,3584]{1,0:T(8,128)(2,1)S(1)}, u32[]{:S(2)}, u32[]{:S(2)}) collective-permute-start(bf16[80,3584]{1,0:T(8,128)(2,1)} %get-tuple-element.84), channel_id=1, source_target_pairs={{0,8},{8,16},{16,24},{24,0},{1,9},{9,17},{17,25},{25,1},{2,10},{10... | collective-permute-start | bytes 1720328 | tf_op jit(solution)/shard_map/cond/branch_1_fun/ppermute | solution.py:16
  140.3 111.3 %collective-permute-start.11 = (bf16[80,3584]{1,0:T(8,128)(2,1)}, bf16[80,3584]{1,0:T(8,128)(2,1)S(1)}, u32[]{:S(2)}, u32[]{:S(2)}) collective-permute-start(bf16[80,3584]{1,0:T(8,128)(2,1)} %get-tuple-element.85), channel_id=1, source_target_pairs={{0,24},{8,0},{16,8},{24,16},{1,25},{9,1},{17,9},{25,17},{2,26},{10... | collective-permute-start | bytes 1720328 | tf_op jit(solution)/shard_map/cond/branch_1_fun/ppermute | solution.py:16
  150.7 122.0 %collective-permute-start.10 = (bf16[80,3584]{1,0:T(8,128)(2,1)}, bf16[80,3584]{1,0:T(8,128)(2,1)S(1)}, u32[]{:S(2)}, u32[]{:S(2)}) collective-permute-start(bf16[80,3584]{1,0:T(8,128)(2,1)} %get-tuple-element.86), channel_id=1, source_target_pairs={{0,16},{8,24},{16,0},{24,8},{1,17},{9,25},{17,1},{25,9},{2,18},{10... | collective-permute-start | bytes 1720328 | tf_op jit(solution)/shard_map/cond/branch_1_fun/ppermute | solution.py:16
  251.5 0.8 copy-start.3
  275.7 47.3 %copy-start.7 = (pred[512]{0:T(512)(128)(4,1)S(1)}, pred[512]{0:T(512)(128)(4,1)}, u32[]{:S(2)}) copy-start(pred[512]{0:T(512)(128)(4,1)} %copy-done.6) | copy-start | bytes 1540
  275.7 47.3 %copy-start.9 = (s32[512]{0:T(512)S(1)}, s32[512]{0:T(512)}, u32[]{:S(2)}) copy-start(s32[512]{0:T(512)} %copy-done.8) | copy-start | bytes 6148
  275.8 135.3 %all-gather.14.cloned.1.call-start = ((), (), s32[]{:S(2)}) async-start(), calls=%async_computation.9 | async-start | bytes 5734400 | tf_op jit(solution)/shard_map/cond/branch_1_fun/all_gather | solution.py:38
  276.9 259.1 %reduce-scatter.9.cloned.1.call-start = ((), (), s32[]{:S(2)}) async-start(), calls=%async_computation.10 | async-start | bytes 4718592 | tf_op jit(solution)/shard_map/cond/branch_1_fun/reduce_scatter | solution.py:39
  340.5 196.6 %reduce-scatter.11.cloned.1.call-start = ((), (), s32[]{:S(2)}) async-start(), calls=%async_computation.11 | async-start | bytes 4718592 | tf_op jit(solution)/shard_map/cond/branch_1_fun/reduce_scatter | solution.py:48
  439.6 1.6 copy-start.10
  439.6 14.2 %slice-start = ((s8[4587520]{0:T(1024)(128)(4,1)}), s8[393216]{0:T(1024)(128)(4,1)S(1)}, s32[]{:S(2)}) async-start(s8[4587520]{0:T(1024)(128)(4,1)} %bitcast.48), calls=%async_computation.14 | async-start | bytes 786432
  441.3 12.6 %slice-start.1 = ((s8[4587520]{0:T(1024)(128)(4,1)}), s8[4194304]{0:T(1024)(128)(4,1)S(1)}, s32[]{:S(2)}) async-start(s8[4587520]{0:T(1024)(128)(4,1)} %bitcast.48), calls=%async_computation.15 | async-start | bytes 8388608
  441.3 12.6 %copy-start.17 = (bf16[320,2048]{1,0:T(8,128)(2,1)S(1)}, bf16[320,2048]{1,0:T(8,128)(2,1)}, u32[]{:S(2)}) copy-start(bf16[320,2048]{1,0:T(8,128)(2,1)} %copy-done.16) | copy-start | bytes 3932164
  538.6 0.7 copy-start.4
  538.6 0.8 copy-start.5
Sparse Core Ops, SparseCore 0:
  9.9 30.4 all-gather.15
  42.3 27.7 all-gather.17
  275.9 47.0 all-gather.11
  325.0 85.9 all-gather.13
  414.2 49.5 reduce-scatter.8
  467.1 51.1 reduce-scatter.10
where the time goes:
time: 557 us; the launch traced here: 547 us
  waiting for transfers between devices  241 us (43%)
  matrix products  104 us (19%)
  local copies, waits for them, and re-layouts  97.4 us (17%)
  starting transfers between devices  58.7 us (11%)
  between operations  15.3 us (3%)
  blocking collectives  12.8 us (2%)
  other arithmetic  9.84 us (2%)
  loops' own time  7.87 us (1%)
    ppermute x6, waiting for transfers between devices, exchange(): received.append(lax.ppermute(block, axis, moves))  76.4 us
    all_gather x1, waiting for transfers between devices, block_terms(): d_projected = lax.all_gather(d_local, 'row', axis=0, tiled=True)  70.2 us
    reshape x1, local copies, waits for them, and re-layouts, block_terms(): return (mixed, d_down, d_in.reshape(in_weight.shape), d_tokens)  62.7 us
    ppermute x6, starting transfers between devices, exchange(): received.append(lax.ppermute(block, axis, moves))  58 us
    all_gather x1, waiting for transfers between devices, block_terms(): hidden_all = lax.all_gather(hidden, 'row', axis=0, tiled=True)  45.8 us
    unnamed x33, local copies, waits for them, and re-layouts  30.9 us
    all_gather x1, waiting for transfers between devices, per_device(): cotangent_all = lax.all_gather(d_mixed, 'col', axis=0, tiled=True)  29.7 us
    dot_general x1, matrix products, block_terms(): jnp.einsum('tk,dk->td', spread(d_projected), flat_in, preferred_element_t...  22 us
  transfers between devices with their start and end apart: 12, of which 7 were waited for; matrix products, arithmetic and copies ran while one was open for 29% of the time, Pallas kernels for 0%

commit v1 on v0

--- a/solution.py
+++ b/solution.py
@@ -34,7 +34,12 @@
     hidden = (activated * up_part).astype(jnp.bfloat16)
     d_gate = d_hidden * up_part * (sigmoid_gate + gate_part * sigmoid_gate * (1.0 - sigmoid_gate))
     d_local = jnp.concatenate([d_gate, d_hidden * activated], 1).astype(jnp.bfloat16)
-    hidden_all = lax.all_gather(hidden, "row", axis=0, tiled=True)
+    ring = [hidden]
+    for hop in range(3):
+        ring.append(lax.ppermute(ring[-1], "row", [(dev, (dev + 1) % 4) for dev in range(4)]))
+    hidden_all = jnp.roll(
+        jnp.concatenate(ring[::-1], axis=0), (lax.axis_index("row") + 1) * ring[0].shape[0], axis=0
+    )
     d_projected = lax.all_gather(d_local, "row", axis=0, tiled=True)
     mixed = lax.psum_scatter(
         jnp.dot(spread(hidden_all), down_weight, preferred_element_type=jnp.float32),

time: 557 us -> 536 us (0.962)
  waiting for transfers between devices: 241 us -> 218 us
    ppermute x0 -> x3, waiting for transfers between devices: none -> 62 us  [block_terms(): lax.ppermute(ring[-1], 'row', [(dev, (dev + 1) % 4) for dev in range(4)])]
    all_gather x1 -> x0, waiting for transfers between devices: 45.8 us -> none  [block_terms(): hidden_all = lax.all_gather(hidden, 'row', axis=0, tiled=True)]
    all_gather x1, waiting for transfers between devices: 70.2 us -> 30.9 us  [block_terms(): d_projected = lax.all_gather(d_local, 'row', axis=0, tiled=True)]
    unnamed x33 -> x40, local copies, waits for them, and re-layouts: 30.9 us -> 33.1 us
  transfers between devices with their start and end apart: 12 -> 14, of which waited for: 7 -> 9; matrix products, arithmetic and copies ran while one was open for 29% -> 32% of each run, Pallas kernels for 0% -> 0%
where the time goes in v1:
time: 536 us; the launch traced here: 527 us
  waiting for transfers between devices  218 us (41%)
  matrix products  104 us (19%)
  local copies, waits for them, and re-layouts  100 us (19%)
  starting transfers between devices  58.7 us (11%)
  between operations  16.4 us (3%)
  blocking collectives  12.8 us (2%)
  other arithmetic  9 us (2%)
  loops' own time  8.07 us (2%)
    ppermute x6, waiting for transfers between devices, exchange(): received.append(lax.ppermute(block, axis, moves))  76.5 us
    reshape x1, local copies, waits for them, and re-layouts, block_terms(): return (mixed, d_down, d_in.reshape(in_weight.shape), d_tokens)  62.5 us
    ppermute x3, waiting for transfers between devices, block_terms(): lax.ppermute(ring[-1], 'row', [(dev, (dev + 1) % 4) for dev in range(4)])  62 us
    ppermute x6, starting transfers between devices, exchange(): received.append(lax.ppermute(block, axis, moves))  58 us
    unnamed x40, local copies, waits for them, and re-layouts  33.1 us
    all_gather x1, waiting for transfers between devices, block_terms(): d_projected = lax.all_gather(d_local, 'row', axis=0, tiled=True)  30.9 us
    all_gather x1, waiting for transfers between devices, per_device(): cotangent_all = lax.all_gather(d_mixed, 'col', axis=0, tiled=True)  29.7 us
    dot_general x1, matrix products, block_terms(): jnp.einsum('tk,dk->td', spread(d_projected), flat_in, preferred_element_t...  21.6 us
  transfers between devices with their start and end apart: 14, of which 9 were waited for; matrix products, arithmetic and copies ran while one was open for 32% of the time, Pallas kernels for 0%

profile of v1, /device:TPU:0, one launch (start us, length us, event | category | flops | bytes accessed | tf_op | source)
XLA Modules:
  0.0 527.2 jit_solution(18251095467633059480)
XLA Ops:
  8.0 0.7 all-gather.10.cloned.1.call-update
  8.8 0.7 all-gather.12.cloned.1.call-update
  9.5 12.8 %all-gather = s32[4,1,128]{2,1,0:T(1,128)S(1)} all-gather(s32[1,1,128]{2,1,0:T(1,128)} %bitcast.43), channel_id=1, replica_groups=mesh['row'=4,'col'=8] {'row'}, dimensions={0}, use_global_device_ids=true | all-gather | bytes 2560 | tf_op jit(solution)/shard_map/all_gather | solution.py:67
  24.2 17.1 %all-gather.10.cloned.1.call-done = bf16[512,2048]{1,0:T(8,128)(2,1)} async-done(((bf16[64,2048]{1,0:T(8,128)(2,1)}), bf16[512,2048]{1,0:T(8,128)(2,1)}) %all-gather.10.cloned.1.call-update) | async-done | bytes 2097168 | tf_op jit(solution)/shard_map/all_gather | solution.py:66
  41.2 29.7 %all-gather.12.cloned.1.call-done = bf16[512,2048]{1,0:T(8,128)(2,1)} async-done(((bf16[64,2048]{1,0:T(8,128)(2,1)}), bf16[512,2048]{1,0:T(8,128)(2,1)}) %all-gather.12.cloned.1.call-update) | async-done | bytes 2097168 | tf_op jit(solution)/shard_map/all_gather | solution.py:65
  70.9 447.8 %conditional.4 = (bf16[3584,2048]{1,0:T(8,128)(2,1)}, bf16[2048,2,3584]{2,1,0:T(2,128)(2,1)}, bf16[64,2048]{1,0:T(8,128)(2,1)S(1)}, bf16[64,2048]{1,0:T(8,128)(2,1)S(1)}) conditional(s32[]{:T(128)} %bitcast.3, (pred[512]{0:T(512)(128)(4,1)S(1)}, bf16[512,2048]{1,0:T(8,128)(2,1)}, bf16[2048,2,3584]{2,1,0:T(2,128)(2,1)}, bf16[512,2048]{1,0:T(8,128)(2,1)}, ...), branch_computations={%region_2.5_spmd, %region_5.8_spmd} | conditional | flops 67683221504 | bytes 554441344
  78.5 20.9 %copy.10 = bf16[256,8,2,3584]{3,1,2,0:T(8,128)(2,1)} copy(bf16[256,8,2,3584]{3,2,1,0:T(2,128)(2,1)} %bitcast.36) | data formatting | bytes 58720256
  99.4 0.8 convolution_convert_fusion.5
  100.2 1.1 copy-done.16
  101.3 14.7 %fusion.45 = f32[320,7168]{1,0:T(8,128)S(1)} fusion(bf16[320,2048]{1,0:T(8,128)(2,1)S(1)} %convolution_convert_fusion.5, bf16[2048,7168]{1,0:T(8,128)(2,1)} %bitcast.39), kind=kOutput, calls=%fused_computation.88 | convolution fusion | flops 9395240960 | bytes 39845888 | tf_op jit(solution)/shard_map/cond/branch_1_fun/dot_general | solution.py:29
  116.0 1.8 dynamic-slice_convert_fusion.8
  117.8 1.5 collective-permute-start.9
  119.3 2.3 collective-permute-start.11
  122.2 1.9 convolution_convert_fusion.4
  124.2 8.6 %fusion.46 = f32[320,3584]{1,0:T(8,128)S(1)} fusion(bf16[320,2048]{1,0:T(8,128)(2,1)} %convolution_convert_fusion.4, bf16[3584,2048]{1,0:T(8,128)(2,1)} %get-tuple-element.49), kind=kOutput, calls=%fused_computation.89 | convolution fusion | flops 4697620480 | bytes 20578304 | tf_op jit(solution)/shard_map/cond/branch_1_fun/td,fd->tf/dot_general | solution.py:27
  132.8 2.1 copy-done.2
  134.9 1.2 dynamic-slice_convert_fusion.11
  136.0 1.5 collective-permute-start.15
  137.5 2.3 collective-permute-start.17
  139.9 8.2 %collective-permute-done.9 = bf16[80,7168]{1,0:T(8,128)(2,1)} collective-permute-done((bf16[80,7168]{1,0:T(8,128)(2,1)}, bf16[80,7168]{1,0:T(8,128)(2,1)}, u32[]{:S(2)}, u32[]{:S(2)}) %collective-permute-start.9) | collective-permute-done | bytes 1146912 | tf_op jit(solution)/shard_map/cond/branch_1_fun/ppermute | solution.py:16
  148.1 49.7 %collective-permute-start.16 = (bf16[80,3584]{1,0:T(8,128)(2,1)S(1)}, bf16[80,3584]{1,0:T(8,128)(2,1)S(1)}, u32[]{:S(2)}, u32[]{:S(2)}) collective-permute-start(bf16[80,3584]{1,0:T(8,128)(2,1)S(1)} %get-tuple-element.86), channel_id=1, source_target_pairs={{0,16},{8,24},{16,0},{24,8},{1,17},{9,25},{17,1},{25,9},{2,18},{10... | collective-permute-start | bytes 1720328 | tf_op jit(solution)/shard_map/cond/branch_1_fun/ppermute | solution.py:16
  197.8 47.9 %collective-permute-done.10 = bf16[80,7168]{1,0:T(8,128)(2,1)} collective-permute-done((bf16[80,7168]{1,0:T(8,128)(2,1)S(1)}, bf16[80,7168]{1,0:T(8,128)(2,1)}, u32[]{:S(2)}, u32[]{:S(2)}) %collective-permute-start.10) | collective-permute-done | bytes 1146912 | tf_op jit(solution)/shard_map/cond/branch_1_fun/ppermute | solution.py:16
  245.7 3.2 convert_add_fusion.2
  248.9 0.8 copy-done.3
  249.7 20.4 %collective-permute-done.16 = bf16[80,3584]{1,0:T(8,128)(2,1)S(1)} collective-permute-done((bf16[80,3584]{1,0:T(8,128)(2,1)S(1)}, bf16[80,3584]{1,0:T(8,128)(2,1)S(1)}, u32[]{:S(2)}, u32[]{:S(2)}) %collective-permute-start.16) | collective-permute-done | bytes 573472 | tf_op jit(solution)/shard_map/cond/branch_1_fun/ppermute | solution.py:16
  270.1 2.2 multiply_convert_fusion.4
  272.3 16.7 %collective-permute-done.12 = bf16[80,3584]{1,0:T(8,128)(2,1)S(1)} collective-permute-done((bf16[80,3584]{1,0:T(8,128)(2,1)S(1)}, bf16[80,3584]{1,0:T(8,128)(2,1)S(1)}, u32[]{:S(2)}, u32[]{:S(2)}) %collective-permute-start.12) | collective-permute-done | bytes 573472 | tf_op jit(solution)/shard_map/cond/branch_1_fun/ppermute | solution.py:39
  289.0 1.1 pad_maximum_fusion.1
  290.2 17.0 %collective-permute-done.13 = bf16[80,3584]{1,0:T(8,128)(2,1)S(1)} collective-permute-done((bf16[80,3584]{1,0:T(8,128)(2,1)S(1)}, bf16[80,3584]{1,0:T(8,128)(2,1)S(1)}, u32[]{:S(2)}, u32[]{:S(2)}) %collective-permute-start.13) | collective-permute-done | bytes 573472 | tf_op jit(solution)/shard_map/cond/branch_1_fun/ppermute | solution.py:39
  307.4 28.3 %collective-permute-done.14 = bf16[80,3584]{1,0:T(8,128)(2,1)S(1)} collective-permute-done((bf16[80,3584]{1,0:T(8,128)(2,1)S(1)}, bf16[80,3584]{1,0:T(8,128)(2,1)S(1)}, u32[]{:S(2)}, u32[]{:S(2)}) %collective-permute-start.14) | collective-permute-done | bytes 573472 | tf_op jit(solution)/shard_map/cond/branch_1_fun/ppermute | solution.py:39
  335.7 0.9 constant_dynamic-update-slice_fusion.15
  336.6 0.9 constant_dynamic-update-slice_fusion.14
  337.5 0.8 constant_dynamic-update-slice_fusion.13
  338.3 0.8 constant_dynamic-update-slice_fusion.12
  339.1 0.8 constant_dynamic-update-slice_fusion.11
  340.0 0.9 constant_dynamic-update-slice_fusion.10
  340.9 0.9 constant_dynamic-update-slice_fusion.9
  341.9 0.8 constant_dynamic-update-slice_fusion.8
  342.7 17.7 %fusion.16 = f32[512,2048]{1,0:T(8,128)} fusion(bf16[3584,2048]{1,0:T(8,128)(2,1)} %get-tuple-element.49, bf16[640,3584]{1,0:T(8,128)(2,1)} %constant_dynamic-update-slice_fusion.8, s32[]{:T(128)S(6)} %select_n.54, s32[512]{0:T(512)S(1)} %copy-done.10, pred[512]{0:T(512)(128)(4,1)S(1)} %copy-done.8), kind=kOutput, calls=%fused_computation.42 | convolution fusion | flops 8692760576 | bytes 21170692 | tf_op jit(solution)/shard_map/cond/branch_1_fun/dot_general | solution.py:45
  360.7 30.9 %all-gather.8.cloned.1.call-done = bf16[320,7168]{1,0:T(8,128)(2,1)} async-done(((bf16[80,7168]{1,0:T(8,128)(2,1)}), bf16[320,7168]{1,0:T(8,128)(2,1)}) %all-gather.8.cloned.1.call-update) | async-done | bytes 4587536 | tf_op jit(solution)/shard_map/cond/branch_1_fun/all_gather | solution.py:43
  391.6 6.6 %convolution_convert_fusion.2.clone.4 = bf16[512,7168]{1,0:T(8,128)(2,1)S(1)} fusion(bf16[320,7168]{1,0:T(8,128)(2,1)} %all-gather.8.cloned.1.call-done, s32[512]{0:T(512)S(1)} %copy-done.10, pred[512]{0:T(512)(128)(4,1)S(1)} %copy-done.8), kind=kOutput, calls=%fused_computation.40.clone.clone.clone.1 | convolution fusion | flops 2352807936 | bytes 11930112 | tf_op jit(solution)/shard_map/cond/branch_1_fun/ct,cf->tf/dot_general | solution.py:77
  398.2 21.6 %fusion.21 = f32[512,2048]{1,0:T(8,128)} fusion(bf16[2048,7168]{1,0:T(8,128)(2,1)} %bitcast.40, bf16[512,7168]{1,0:T(8,128)(2,1)S(1)} %convolution_convert_fusion.2.clone.4), kind=kOutput, calls=%fused_computation.52 | convolution fusion | flops 15032385536 | bytes 40894464 | tf_op jit(solution)/shard_map/cond/branch_1_fun/tk,dk->td/dot_general | solution.py:54
  419.8 1.3 copy-done.18
  421.1 13.2 %fusion.19 = bf16[3584,2048]{1,0:T(8,128)(2,1)} fusion(bf16[320,2048]{1,0:T(8,128)(2,1)S(1)} %copy-done.18, bf16[640,3584]{1,0:T(8,128)(2,1)} %constant_dynamic-update-slice_fusion.8, s32[]{:T(128)S(6)} %select_n.54), kind=kOutput, calls=%fused_computation.50 | convolution fusion | flops 4697620480 | bytes 18284548 | tf_op jit(solution)/shard_map/cond/branch_1_fun/tf,td->fd/dot_general | solution.py:50
  434.2 19.5 %convolution_convert_fusion.1 = bf16[2048,7168]{1,0:T(8,128)(2,1)} fusion(bf16[320,2048]{1,0:T(8,128)(2,1)S(1)} %copy-done.17, bf16[320,7168]{1,0:T(8,128)(2,1)S(1)} %bitcast.45), kind=kOutput, calls=%fused_computation.39 | convolution fusion | flops 9409921024 | bytes 35258368 | tf_op jit(solution)/shard_map/cond/branch_1_fun/td,tk->dk/dot_general | solution.py:59
  453.7 62.5 %reshape.42 = bf16[2048,2,3584]{2,1,0:T(2,128)(2,1)} reshape(bf16[2048,7168]{1,0:T(8,128)(2,1)} %convolution_convert_fusion.1) | data formatting | bytes 58720256 | tf_op jit(solution)/shard_map/cond/branch_1_fun/reshape | solution.py:61
  516.2 1.1 convert_element_type.146
  517.3 1.1 convert_element_type.148
  (54 shorter events, 3.5 us)
Async XLA Ops:
  8.0 33.2 %all-gather.10.cloned.1.call-start = ((), (), s32[]{:S(2)}) async-start(), calls=%async_computation.10 | async-start | bytes 2359296 | tf_op jit(solution)/shard_map/all_gather | solution.py:66
  8.7 62.2 %all-gather.12.cloned.1.call-start = ((), (), s32[]{:S(2)}) async-start(), calls=%async_computation.11 | async-start | bytes 2359296 | tf_op jit(solution)/shard_map/all_gather | solution.py:65
  78.4 43.8 %copy-start.7 = (pred[512]{0:T(512)(128)(4,1)}, pred[512]{0:T(512)(128)(4,1)S(1)}, u32[]{:S(2)}) copy-start(pred[512]{0:T(512)(128)(4,1)S(1)} %get-tuple-element.44) | copy-start | bytes 1540
  78.4 43.8 %copy-start.9 = (s32[512]{0:T(512)}, s32[512]{0:T(512)S(1)}, u32[]{:S(2)}) copy-start(s32[512]{0:T(512)S(1)} %get-tuple-element.45) | copy-start | bytes 6148
  78.4 313.2 %all-gather.8.cloned.1.call-start = ((), (), s32[]{:S(2)}) async-start(), calls=%async_computation.7 | async-start | bytes 5734400 | tf_op jit(solution)/shard_map/cond/branch_1_fun/all_gather | solution.py:43
  78.5 20.9 %copy-start.13 = (bf16[512,2048]{1,0:T(8,128)(2,1)S(1)}, bf16[512,2048]{1,0:T(8,128)(2,1)}, u32[]{:S(2)}) copy-start(bf16[512,2048]{1,0:T(8,128)(2,1)} %get-tuple-element.46) | copy-start | bytes 6291460
  100.2 1.1 copy-start.16
  116.0 8.2 %copy-start = (f32[320,7168]{1,0:T(8,128)}, f32[320,7168]{1,0:T(8,128)S(1)}, u32[]{:S(2)}) copy-start(f32[320,7168]{1,0:T(8,128)S(1)} %fusion.45) | copy-start | bytes 27525124
  116.0 6.2 %copy-start.15 = (bf16[512,2048]{1,0:T(8,128)(2,1)S(1)}, bf16[512,2048]{1,0:T(8,128)(2,1)}, u32[]{:S(2)}) copy-start(bf16[512,2048]{1,0:T(8,128)(2,1)} %get-tuple-element.48) | copy-start | bytes 6291460
  117.8 30.3 %collective-permute-start.9 = (bf16[80,7168]{1,0:T(8,128)(2,1)}, bf16[80,7168]{1,0:T(8,128)(2,1)}, u32[]{:S(2)}, u32[]{:S(2)}) collective-permute-start(bf16[80,7168]{1,0:T(8,128)(2,1)} %get-tuple-element.79), channel_id=1, source_target_pairs={{0,8},{8,16},{16,24},{24,0},{1,9},{9,17},{17,25},{25,1},{2,10},{10... | collective-permute-start | bytes 3440648 | tf_op jit(solution)/shard_map/cond/branch_1_fun/ppermute | solution.py:16
  119.3 78.5 %collective-permute-start.11 = (bf16[80,7168]{1,0:T(8,128)(2,1)}, bf16[80,7168]{1,0:T(8,128)(2,1)}, u32[]{:S(2)}, u32[]{:S(2)}) collective-permute-start(bf16[80,7168]{1,0:T(8,128)(2,1)} %get-tuple-element.80), channel_id=1, source_target_pairs={{0,24},{8,0},{16,8},{24,16},{1,25},{9,1},{17,9},{25,17},{2,26},{10... | collective-permute-start | bytes 3440648 | tf_op jit(solution)/shard_map/cond/branch_1_fun/ppermute | solution.py:16
  121.6 124.1 %collective-permute-start.10 = (bf16[80,7168]{1,0:T(8,128)(2,1)S(1)}, bf16[80,7168]{1,0:T(8,128)(2,1)}, u32[]{:S(2)}, u32[]{:S(2)}) collective-permute-start(bf16[80,7168]{1,0:T(8,128)(2,1)S(1)} %get-tuple-element.81), channel_id=1, source_target_pairs={{0,16},{8,24},{16,0},{24,8},{1,17},{9,25},{17,1},{25,9},{2,18},{10... | collective-permute-start | bytes 3440648 | tf_op jit(solution)/shard_map/cond/branch_1_fun/ppermute | solution.py:16
  132.8 2.1 copy-start.2
  136.0 112.8 %collective-permute-start.15 = (bf16[80,3584]{1,0:T(8,128)(2,1)}, bf16[80,3584]{1,0:T(8,128)(2,1)S(1)}, u32[]{:S(2)}, u32[]{:S(2)}) collective-permute-start(bf16[80,3584]{1,0:T(8,128)(2,1)} %get-tuple-element.84), channel_id=1, source_target_pairs={{0,8},{8,16},{16,24},{24,0},{1,9},{9,17},{17,25},{25,1},{2,10},{10... | collective-permute-start | bytes 1720328 | tf_op jit(solution)/shard_map/cond/branch_1_fun/ppermute | solution.py:16
  137.5 111.3 %collective-permute-start.17 = (bf16[80,3584]{1,0:T(8,128)(2,1)}, bf16[80,3584]{1,0:T(8,128)(2,1)S(1)}, u32[]{:S(2)}, u32[]{:S(2)}) collective-permute-start(bf16[80,3584]{1,0:T(8,128)(2,1)} %get-tuple-element.85), channel_id=1, source_target_pairs={{0,24},{8,0},{16,8},{24,16},{1,25},{9,1},{17,9},{25,17},{2,26},{10... | collective-permute-start | bytes 1720328 | tf_op jit(solution)/shard_map/cond/branch_1_fun/ppermute | solution.py:16
  148.1 122.0 %collective-permute-start.16 = (bf16[80,3584]{1,0:T(8,128)(2,1)S(1)}, bf16[80,3584]{1,0:T(8,128)(2,1)S(1)}, u32[]{:S(2)}, u32[]{:S(2)}) collective-permute-start(bf16[80,3584]{1,0:T(8,128)(2,1)S(1)} %get-tuple-element.86), channel_id=1, source_target_pairs={{0,16},{8,24},{16,0},{24,8},{1,17},{9,25},{17,1},{25,9},{2,18},{10... | collective-permute-start | bytes 1720328 | tf_op jit(solution)/shard_map/cond/branch_1_fun/ppermute | solution.py:16
  248.9 0.8 copy-start.3
  272.2 16.7 %collective-permute-start.12 = (bf16[80,3584]{1,0:T(8,128)(2,1)S(1)}, bf16[80,3584]{1,0:T(8,128)(2,1)S(1)}, u32[]{:S(2)}, u32[]{:S(2)}) collective-permute-start(bf16[80,3584]{1,0:T(8,128)(2,1)S(1)} %get-tuple-element.87), channel_id=1, source_target_pairs={{0,8},{8,16},{16,24},{24,0},{1,9},{9,17},{17,25},{25,1},{2,10},{10... | collective-permute-start | bytes 1720328 | tf_op jit(solution)/shard_map/cond/branch_1_fun/ppermute | solution.py:39
  289.0 18.2 %collective-permute-start.13 = (bf16[80,3584]{1,0:T(8,128)(2,1)S(1)}, bf16[80,3584]{1,0:T(8,128)(2,1)S(1)}, u32[]{:S(2)}, u32[]{:S(2)}) collective-permute-start(bf16[80,3584]{1,0:T(8,128)(2,1)S(1)} %collective-permute-done.12), channel_id=1, source_target_pairs={{0,8},{8,16},{16,24},{24,0},{1,9},{9,17},{17,25},{25,1},{2,10},{10... | collective-permute-start | bytes 1720328 | tf_op jit(solution)/shard_map/cond/branch_1_fun/ppermute | solution.py:39
  290.1 226.1 %reduce-scatter.9.cloned.1.call-start = ((), (), s32[]{:S(2)}) async-start(), calls=%async_computation.8 | async-start | bytes 4718592 | tf_op jit(solution)/shard_map/cond/branch_1_fun/reduce_scatter | solution.py:44
  307.2 28.5 %collective-permute-start.14 = (bf16[80,3584]{1,0:T(8,128)(2,1)S(1)}, bf16[80,3584]{1,0:T(8,128)(2,1)S(1)}, u32[]{:S(2)}, u32[]{:S(2)}) collective-permute-start(bf16[80,3584]{1,0:T(8,128)(2,1)S(1)} %collective-permute-done.13), channel_id=1, source_target_pairs={{0,8},{8,16},{16,24},{24,0},{1,9},{9,17},{17,25},{25,1},{2,10},{10... | collective-permute-start | bytes 1720328 | tf_op jit(solution)/shard_map/cond/branch_1_fun/ppermute | solution.py:39
  337.4 5.2 copy-start.8
  337.5 5.2 copy-start.10
  360.4 156.9 %reduce-scatter.11.cloned.1.call-start = ((), (), s32[]{:S(2)}) async-start(), calls=%async_computation.9 | async-start | bytes 4718592 | tf_op jit(solution)/shard_map/cond/branch_1_fun/reduce_scatter | solution.py:53
  419.7 1.3 copy-start.18
  419.7 14.5 %slice-start = ((s8[4587520]{0:T(1024)(128)(4,1)}), s8[393216]{0:T(1024)(128)(4,1)S(1)}, s32[]{:S(2)}) async-start(s8[4587520]{0:T(1024)(128)(4,1)} %bitcast.44), calls=%async_computation.12 | async-start | bytes 786432
  421.1 13.2 %slice-start.1 = ((s8[4587520]{0:T(1024)(128)(4,1)}), s8[4194304]{0:T(1024)(128)(4,1)S(1)}, s32[]{:S(2)}) async-start(s8[4587520]{0:T(1024)(128)(4,1)} %bitcast.44), calls=%async_computation.13 | async-start | bytes 8388608
  421.1 13.2 %copy-start.17 = (bf16[320,2048]{1,0:T(8,128)(2,1)S(1)}, bf16[320,2048]{1,0:T(8,128)(2,1)}, u32[]{:S(2)}) copy-start(bf16[320,2048]{1,0:T(8,128)(2,1)} %copy-done.16) | copy-start | bytes 3932164
  518.7 0.7 copy-start.4
  518.7 0.8 copy-start.5
Sparse Core Ops, SparseCore 0:
  10.7 30.4 all-gather.9
  43.1 27.7 all-gather.11
  290.2 101.3 all-gather.7
Sparse Core Ops, SparseCore 1:
  360.5 59.4 reduce-scatter.8
  423.1 51.0 reduce-scatter.10
